TPU v7x, 32 devices: a whole 2x2x4 slice. The times are simulated.
32 devices in a mesh: patch: 2 (over y), epoch: 4 (over z), tile: 4 (over x, core).
Axes of the slice: x: 2, y: 2, z: 4, core: 2. Of those that a mesh axis runs over, the one named last changes fastest.
Arguments:
- template: float32 [768, 512], P(('patch', 'epoch'), 'tile'), parts along dimension 0, may hold values from -14.2 to 14.2
- science: float32 [8, 384, 512], P(('patch', 'epoch'), None, 'tile'), parts along dimension 0, may hold values from -31 to 31
- row_profiles: float32 [12, 21], replicated, may hold values from -1.25 to 1.25
- col_profiles: float32 [12, 21], replicated, may hold values from -1.25 to 1.25
- coverage: int32 [8, 256], P(('patch', 'epoch'), 'tile'), parts along dimension 0, may hold values 0 or 1
- stamp_rows: int32 [512], P(('patch', 'tile')), parts along dimension 0, may hold values from 0 to 352
- stamp_cols: int32 [512], P(('patch', 'tile')), parts along dimension 0, may hold values from 0 to 96
Outputs:
- difference: float32 [8, 384, 512], P(('patch', 'epoch'), None, 'tile'), parts along dimension 0
There are 2 independent parts, one for each index of `patch`. A program takes and returns all parts, laid end to end along the dimension named above; an argument that names none is the same for every part. Nothing has to cross between parts.
All inputs are finite; a program needn't handle non-finite values. No bound on the sum of `coverage` on one device may be relied on, other than what follows from the above.
Results may differ from a plain program's by a relative error of at most 0.00011.
Values sent between devices are 32-bit elements; how exact they have to be, the bound alone decides.
A program may use at most 128 MiB of HBM per device.

v0:
```python
import functools

import jax
import jax.numpy as jnp
from jax import lax
from jax.experimental import pallas as pl
from jax.experimental.pallas import tpu as pltpu
from jax.sharding import PartitionSpec as P

S = 32
GROUP = 16
EDGE = 16
CHUNK = 64
LANES = 128
ridge_weight = 1.0
F32 = jnp.float32
BF16 = jnp.bfloat16
NT = (((1,), (1,)), ((), ()))
NN = (((1,), (0,)), ((), ()))


def split(value):
    high = value.astype(BF16)
    return high, (value - high.astype(F32)).astype(BF16)


def toeplitz(profile_row, rows, shift, width):
    base = pltpu.roll(jnp.broadcast_to(profile_row, (8, width)), 0, 1, stride=1, stride_axis=0)
    turns = [(shift + first) % width for first in range(0, rows, 8)]
    return jnp.concatenate([pltpu.roll(base, turn, 1) if turn else base for turn in turns], axis=0)


def iota(shape, axis):
    return lax.broadcasted_iota(jnp.int32, shape, axis)


def row_block(rows, extra, width):
    best = 8
    for size in range(8, width - extra + 1, 8):
        if rows % size == 0:
            best = size
    return best


def xi_row(cols, total):
    start = lax.axis_index("tile") * cols
    return 2.0 * (start + iota((1, cols), 1)).astype(F32) / total - 1.0


def make_bands(rowp_ref, colp_ref, profile_ref, row_band_ref, col_band_ref, shift):
    count, taps = rowp_ref.shape
    width = profile_ref.shape[2]
    profile_ref[...] = jnp.zeros_like(profile_ref)
    profile_ref[0, :count, :taps] = rowp_ref[...]
    profile_ref[1, :count, :taps] = colp_ref[...]
    for b in range(count):
        band = split(toeplitz(profile_ref[0, b : b + 1, :], row_band_ref.shape[2], shift, width))
        row_band_ref[0, b], row_band_ref[1, b] = band
        band = split(toeplitz(profile_ref[1, b : b + 1, :], col_band_ref.shape[2], -(taps // 2), width))
        col_band_ref[0, b], col_band_ref[1, b] = band


def column_pass(strip, at, col_band_ref, across_ref):
    count, _, lanes = across_ref.shape
    cols = lanes // 2
    high, low = split(strip)
    dot = functools.partial(lax.dot_general, dimension_numbers=NT, preferred_element_type=F32)
    for pair in range(0, count, 2):
        members = [b for b in (pair, pair + 1) if b < count]
        small = dot(low, jnp.concatenate([col_band_ref[0, b] for b in members], axis=0))
        for k, b in enumerate(members):
            big = dot(high, jnp.concatenate([col_band_ref[0, b], col_band_ref[1, b]], axis=0))
            across = big[:, :cols] + (big[:, cols:] + small[:, k * cols : (k + 1) * cols])
            across_ref[b, at, :] = jnp.concatenate(split(across), axis=1)


def row_pass(row_band_ref, across_ref, images_ref, mixed_ref):
    count, rows, cols = images_ref.shape
    block, width = row_band_ref.shape[2:]
    dot = functools.partial(lax.dot_general, dimension_numbers=NN, preferred_element_type=F32)
    for b in range(count):
        for start in range(0, rows, block):
            across = across_ref[b, start : start + width, :]
            big = dot(row_band_ref[0, b], across)
            small = dot(row_band_ref[1, b], across[:, :cols])
            piece = big[:, :cols] + (big[:, cols:] + small)
            images_ref[b, start : start + block, :] = piece
            mixed_ref[pl.ds(start * GROUP + b, block, stride=GROUP), :] = piece


def chunk_rows(rows):
    return max(size for size in range(1, CHUNK + 1) if rows % size == 0)


def make_weight(srow_ref, scol_ref, cov_ref, weight_ref):
    cols = weight_ref.shape[1]
    stamps = srow_ref.shape[1]
    at = iota((cols, stamps), 0) - scol_ref[...]
    cols_in = jnp.where((at >= 0) & (at < S), cov_ref[...].astype(F32), 0.0).astype(BF16)
    step = chunk_rows(weight_ref.shape[0] // GROUP)
    size = step * GROUP

    def body(chunk, carry):
        at_row = chunk * step + iota((size, 1), 0) // GROUP - srow_ref[...]
        rows_in = jnp.where((at_row >= 0) & (at_row < S), 1.0, 0.0).astype(BF16)
        at = pl.ds(pl.multiple_of(chunk * size, size), size)
        weight_ref[at, :] = lax.dot_general(rows_in, cols_in, NT, preferred_element_type=F32)
        return carry

    lax.fori_loop(0, weight_ref.shape[0] // size, body, 0)


def gram(weight_ref, mixed_ref, total):
    height, cols = mixed_ref.shape
    rows = height // GROUP
    xi = xi_row(cols, total)
    step = chunk_rows(rows)
    size = step * GROUP

    def lay(values):
        return jnp.concatenate(
            [
                jnp.concatenate([v[k * GROUP : (k + 1) * GROUP] for k in range(step)], axis=1)
                for v in values
            ],
            axis=0,
        )

    def body(chunk, acc):
        at = pl.ds(pl.multiple_of(chunk * size, size), size)
        base = mixed_ref[at, :]
        weight = weight_ref[at, :]
        y = chunk * step + iota((size, 1), 0) // GROUP
        eta = 2.0 * y.astype(F32) / rows - 1.0
        feats = (base, base * xi, base * eta)
        right = jnp.concatenate(split(lay(feats)), axis=0)
        left = jnp.concatenate(split(lay([f * weight for f in feats])), axis=0)
        return acc + lax.dot_general(left, right, NT, preferred_element_type=F32)

    side = 3 * GROUP
    sums = lax.fori_loop(0, rows // step, body, jnp.zeros((2 * side, 2 * side), F32))
    return sums[:side, :side] + (sums[:side, side:] + sums[side:, :side] + sums[side:, side:])


def solve(normal, count):
    side = 3 * GROUP
    row, col = iota((side, LANES), 0), iota((side, LANES), 1)

    def used(k):
        return ((k % GROUP < count) & (k < side)) | (k == count)

    rhs = normal[:, count + 1 : count + 2]
    system = jnp.where(used(row) & used(col), normal, 0.0) + ridge_weight * jnp.where(row == col, 1.0, 0.0)
    system = jnp.where((col == side) & used(row), rhs, system)
    unknowns = [k for k in range(side) if (k % GROUP < count) or k == count]
    for p in unknowns:
        pivot_row = system[p : p + 1, :]
        scaled = pivot_row / system[p : p + 1, p : p + 1]
        factor = jnp.where(row[:, :1] == p, 0.0, system[:, p : p + 1])
        system = system - factor * scaled
    diagonal = jnp.sum(jnp.where(row == col, system, 0.0), axis=1, keepdims=True)
    return system[:, side : side + 1] / diagonal


def apply(coefs, images_ref, science_ref, out_ref, total):
    count, rows, cols = images_ref.shape
    xi = xi_row(cols, total)
    eta = 2.0 * iota((rows, 1), 0).astype(F32) / rows - 1.0
    field = jnp.broadcast_to(coefs[count : count + 1, :], (rows, cols))
    for b in range(count):
        flat = coefs[b : b + 1] + coefs[GROUP + b : GROUP + b + 1] * xi
        field = field + images_ref[b] * (flat + coefs[2 * GROUP + b : 2 * GROUP + b + 1] * eta)
    out_ref[0] = science_ref[0] - field


def fill_rest(mixed_ref, science, count):
    rows = science.shape[0]
    mixed_ref[pl.ds(count, rows, stride=GROUP), :] = jnp.ones_like(science)
    mixed_ref[pl.ds(count + 1, rows, stride=GROUP), :] = science
    for spare in range(count + 2, GROUP):
        mixed_ref[pl.ds(spare, rows, stride=GROUP), :] = jnp.zeros_like(science)


def remote(source, target, send, recv, epoch, tile):
    return pltpu.make_async_remote_copy(
        src_ref=source,
        dst_ref=target,
        send_sem=send,
        recv_sem=recv,
        device_id={"epoch": epoch, "tile": tile},
        device_id_type=pl.DeviceIdType.MESH,
    )


def kernel(total, top, template_in, science_in, rowp_in, colp_in, cov_in, srow_in, scol_in, out_ref,
           science_ref, rowp_ref, colp_ref, cov_ref, srow_ref, scol_ref,
           slots, pack, edges, across_ref, parts, mine, images_ref, mixed_ref, weight_ref, profile_ref,
           row_band_ref, col_band_ref, slot_send, slot_recv, edge_send, edge_recv, part_send, part_recv, load_sem):
    count, rows, cols = images_ref.shape
    taps = rowp_ref.shape[1]
    epochs, own_rows, _ = slots.shape
    tiles = parts.shape[0]
    epoch, tile = lax.axis_index("epoch"), lax.axis_index("tile")

    loads = [
        pltpu.make_async_copy(source, target, load_sem.at[k])
        for k, (source, target) in enumerate(
            [
                (template_in, slots.at[epoch]),
                (cov_in, cov_ref),
                (srow_in, srow_ref),
                (scol_in, scol_ref),
                (rowp_in, rowp_ref),
                (colp_in, colp_ref),
                (science_in, science_ref),
            ]
        )
    ]
    for load in loads:
        load.start()
    barrier = pltpu.get_barrier_semaphore()
    for e in range(epochs):
        for t in range(tiles):
            if e or t:
                where = {"epoch": lax.rem(epoch + e, epochs), "tile": lax.rem(tile + t, tiles)}
                pl.semaphore_signal(barrier, inc=1, device_id=where, device_id_type=pl.DeviceIdType.MESH)
    loads[0].wait()
    flipped = jnp.transpose(slots[epoch])
    pack[0] = flipped[:EDGE]
    pack[1] = flipped[cols - EDGE :]
    pl.semaphore_wait(barrier, epochs * tiles - 1)

    def block_copy(e, source):
        return remote(slots.at[epoch], slots.at[source], slot_send.at[e], slot_recv.at[source],
                      lax.rem(epoch + e, epochs), tile)

    def edge_copy(e, side, source):
        beside = tile - 1 if side == 0 else tile + 1
        return remote(pack.at[side], edges.at[side, source], edge_send.at[side, e], edge_recv.at[side, source],
                      lax.rem(epoch + e, epochs), beside)

    has_left, has_right = tile > 0, tile < tiles - 1
    order = sorted(range(epochs), key=lambda e: -e * (epochs - e))
    for e in order:
        if e:
            block_copy(e, epoch).start()

        @pl.when(has_left)
        def _():
            edge_copy(e, 0, epoch).start()

        @pl.when(has_right)
        def _():
            edge_copy(e, 1, epoch).start()

    for load in loads[1:]:
        load.wait()
    make_weight(srow_ref, scol_ref, cov_ref, weight_ref)
    make_bands(rowp_ref, colp_ref, profile_ref, row_band_ref, col_band_ref, top - taps // 2)
    fill_rest(mixed_ref, science_ref[0], count)
    high = across_ref.shape[1]
    across_ref[:, :top, :] = jnp.zeros((count, top, 2 * cols), BF16)
    across_ref[:, top + rows :, :] = jnp.zeros((count, high - top - rows, 2 * cols), BF16)

    @pl.when(tile == tiles - 1)
    def _():
        edges[0] = jnp.zeros(edges.shape[1:], F32)

    @pl.when(tile == 0)
    def _():
        edges[1] = jnp.zeros(edges.shape[1:], F32)

    def arrive(source):
        e = lax.rem(epoch + epochs - source, epochs)

        @pl.when(e != 0)
        def _():
            block_copy(e, source).wait_recv()

        @pl.when(has_left)
        def _():
            edge_copy(e, 1, source).wait_recv()

        @pl.when(has_right)
        def _():
            edge_copy(e, 0, source).wait_recv()

    middle = jnp.zeros((cols - 2 * EDGE, own_rows), F32)

    def strip_of(source):
        beside = jnp.transpose(jnp.concatenate([edges[0, source], middle, edges[1, source]], axis=0))
        return jnp.concatenate([slots[source], beside], axis=1)

    groups = 2 if epochs % 2 == 0 and own_rows % 16 == 0 else 1
    each = epochs // groups
    for turn in range(groups):
        group = lax.rem(epoch // each + turn, groups)
        for k in range(each):
            arrive(group * each + k)
        strip = jnp.concatenate([strip_of(group * each + k) for k in range(each)], axis=0)
        height = each * own_rows
        at = pl.ds(pl.multiple_of(top + group * height, 16), height) if groups > 1 else pl.ds(top, height)
        column_pass(strip, at, col_band_ref, across_ref)
    row_pass(row_band_ref, across_ref, images_ref, mixed_ref)
    normal = gram(weight_ref, mixed_ref, total)
    side = 3 * GROUP
    normal = jnp.concatenate([normal, jnp.zeros((side, LANES - side), F32)], axis=1)
    mine[...] = normal

    def part_copy(t, source):
        return remote(mine, parts.at[source], part_send.at[t], part_recv.at[source],
                      epoch, lax.rem(tile + t, tiles))

    for t in range(1, tiles):
        part_copy(t, tile).start()
    for t in range(1, tiles):
        source = lax.rem(tile + tiles - t, tiles)
        part_copy(t, source).wait_recv()
        normal = normal + parts[source]
    for t in range(1, tiles):
        part_copy(t, tile).wait_send()
    for e in range(epochs):
        if e:
            block_copy(e, epoch).wait_send()

        @pl.when(has_left)
        def _():
            edge_copy(e, 0, epoch).wait_send()

        @pl.when(has_right)
        def _():
            edge_copy(e, 1, epoch).wait_send()

    coefs = solve(normal, count)
    apply(coefs, images_ref, science_ref, out_ref, total)


def local(template, science, row_profiles, col_profiles, coverage, stamp_rows, stamp_cols):
    count, taps = row_profiles.shape
    rows, cols = science.shape[1:]
    own_rows = template.shape[0]
    tiles, epochs = lax.axis_size("tile"), lax.axis_size("epoch")
    width = 2 * LANES
    top = -(-(taps // 2) // 16) * 16
    block = row_block(rows, taps - 1 + top - taps // 2, width)
    vmem = pl.BlockSpec(memory_space=pltpu.VMEM)
    dma = pltpu.SemaphoreType.DMA
    return pl.pallas_call(
        functools.partial(kernel, cols * tiles, top),
        out_shape=jax.ShapeDtypeStruct(science.shape, F32),
        in_specs=[pl.BlockSpec(memory_space=pl.ANY)] * 7,
        out_specs=vmem,
        scratch_shapes=[
            pltpu.VMEM(science.shape, F32),
            pltpu.VMEM(row_profiles.shape, F32),
            pltpu.VMEM(col_profiles.shape, F32),
            pltpu.VMEM(coverage.shape, jnp.int32),
            pltpu.VMEM((1, stamp_rows.shape[0]), jnp.int32),
            pltpu.VMEM((1, stamp_cols.shape[0]), jnp.int32),
            pltpu.VMEM((epochs, own_rows, cols), F32),
            pltpu.VMEM((2, EDGE, own_rows), F32),
            pltpu.VMEM((2, epochs, EDGE, own_rows), F32),
            pltpu.VMEM((count, rows - block + width, 2 * cols), BF16),
            pltpu.VMEM((tiles, 3 * GROUP, LANES), F32),
            pltpu.VMEM((3 * GROUP, LANES), F32),
            pltpu.VMEM((count, rows, cols), F32),
            pltpu.VMEM((rows * GROUP, cols), F32),
            pltpu.VMEM((rows * GROUP, cols), F32),
            pltpu.VMEM((2, GROUP, width), F32),
            pltpu.VMEM((2, count, block, width), BF16),
            pltpu.VMEM((2, count, cols, width), BF16),
            dma((epochs,)),
            dma((epochs,)),
            dma((2, epochs)),
            dma((2, epochs)),
            dma((tiles,)),
            dma((tiles,)),
            dma((7,)),
        ],
        compiler_params=pltpu.CompilerParams(
            collective_id=0, has_side_effects=True, vmem_limit_bytes=63 * 2**20
        ),
    )(
        template,
        science,
        row_profiles,
        col_profiles,
        coverage,
        stamp_rows.reshape(1, -1),
        stamp_cols.reshape(1, -1),
    )


def solution(mesh):
    in_specs = (
        P(("patch", "epoch"), "tile"),
        P(("patch", "epoch"), None, "tile"),
        P(),
        P(),
        P(("patch", "epoch"), "tile"),
        P(("patch", "tile")),
        P(("patch", "tile")),
    )
    out_specs = P(("patch", "epoch"), None, "tile")
    return jax.shard_map(local, mesh=mesh, in_specs=in_specs, out_specs=out_specs, check_vma=False)
```

profile of v0, /device:TPU:0, one launch (start us, length us, event | category | flops | bytes accessed | tf_op | source)
XLA Modules:
  0.0 28.4 jit_solution(4581177154298112802)
XLA Ops:
  0.0 26.7 %shard_map.73 = f32[1,384,128]{2,1,0:T(8,128)} custom-call(f32[96,128]{1,0:T(8,128)} %template_in.1, f32[1,384,128]{2,1,0:T(8,128)} %science_in.1, f32[12,21]{1,0:T(8,128)} %rowp_in.1, f32[12,21]{1,0:T(8,128)} %colp_in.1, s32[1,64]{1,0:T(1,128)} %cov_in.1, s32[1,64]{1,0:T(1,128)} %bitcast.2, s32[1,64]{1,0:T(1,128)} %bitcast.3), custom_call_target="tpu_custom_call" | custom-call | tf_op jit(solution)/shard_map/pallas_call | solution.py:348
  26.7 1.6 %copy.9 = f32[1,384,128]{2,1,0:T(8,128)} copy(f32[1,384,128]{2,1,0:T(8,128)} %shard_map.73) | data formatting | bytes 393216
where the time goes:
time: 28.5 us; the launch traced here: 28.4 us
  Pallas kernels  26.7 us (94%)
  local copies, waits for them, and re-layouts  1.62 us (6%)
    pallas_call x1, Pallas kernels, local(): pl.pallas_call(functools.partial(kernel, cols * tiles, top), out_shape=ja...  26.7 us
    unnamed x1, local copies, waits for them, and re-layouts  1.62 us

commit v1 on v0

v1 whole, which is shorter than its diff:
```python
import functools

import jax
import jax.numpy as jnp
from jax import lax
from jax.experimental import pallas as pl
from jax.experimental.pallas import tpu as pltpu
from jax.sharding import PartitionSpec as P

S = 32
GROUP = 16
EDGE = 16
LANES = 128
HALF = LANES // 2
BLOCK = 8
PIECES = 2
ridge_weight = 1.0
F32 = jnp.float32
BF16 = jnp.bfloat16
NT = (((1,), (1,)), ((), ()))
NN = (((1,), (0,)), ((), ()))


def split(value):
    high = value.astype(BF16)
    return high, (value - high.astype(F32)).astype(BF16)


def iota(shape, axis):
    return lax.broadcasted_iota(jnp.int32, shape, axis)


def shifted(value, turn):
    turn %= value.shape[1]
    return pltpu.roll(value, turn, 1) if turn else value


def toeplitz(profile_row, rows):
    width = profile_row.shape[1]
    base = pltpu.roll(jnp.broadcast_to(profile_row, (8, width)), 0, 1, stride=1, stride_axis=0)
    return jnp.concatenate([shifted(base, first) for first in range(0, rows, 8)], axis=0)


def xi_row(cols, total):
    start = lax.axis_index("tile") * cols
    return 2.0 * (start + iota((1, cols), 1)).astype(F32) / total - 1.0


def chunk_rows(rows, own, extra):
    sizes = [r for r in range(16, LANES - extra + 1, 16) if rows % r == 0 and r % own == 0]
    return max(sizes)


def make_bands(rowp_ref, colp_ref, profile_ref, row_band_ref, col_band_ref, shift):
    count, taps = rowp_ref.shape
    seg = HALF + taps - 1
    profile_ref[...] = jnp.zeros_like(profile_ref)
    high, low = (part.astype(F32) for part in split(rowp_ref[...]))
    profile_ref[0, :count, shift : shift + taps] = high
    profile_ref[0, :count, LANES + shift : LANES + shift + taps] = low
    high, low = (part.astype(F32) for part in split(colp_ref[...]))
    profile_ref[1, :count, :taps] = high
    profile_ref[1, :count, seg : seg + taps] = high
    profile_ref[1, :count, 2 * seg : 2 * seg + taps] = low
    for b in range(count):
        row_band_ref[b] = toeplitz(profile_ref[0, b : b + 1, :], row_band_ref.shape[1]).astype(BF16)
        col_band_ref[b] = toeplitz(profile_ref[1, b : b + 1, :], HALF).astype(BF16)


def window_terms(window, seg):
    lane = iota((1, LANES), 1)
    high = window.astype(BF16).astype(F32)
    low = shifted(window - high, seg)
    first = jnp.where(lane < seg, high, low)
    second = jnp.where(lane < 2 * seg - LANES, low, shifted(high, 2 * seg))
    return jnp.concatenate([first, second], axis=1).astype(BF16)


def column_pass(own, beside, at, taps, col_band_ref, across_ref):
    count = across_ref.shape[0]
    rows = own.shape[0]
    half = taps // 2
    seg = HALF + taps - 1
    lane = iota((1, LANES), 1)
    left = jnp.where(lane < half, shifted(beside, half - EDGE), jnp.where(lane < seg, shifted(own, half), 0.0))
    cut = HALF + half
    right = jnp.where(lane < cut, shifted(own, half - HALF), jnp.where(lane < seg, shifted(beside, cut - EDGE), 0.0))
    terms = jnp.concatenate([window_terms(left, seg), window_terms(right, seg)], axis=0)
    for first in range(0, count, 4):
        members = [b for b in range(first, first + 4) if b < count]
        band = jnp.concatenate([col_band_ref[b] for b in members], axis=0)
        both = lax.dot_general(terms, band, NT, preferred_element_type=F32)
        for k in range(0, len(members), 2):
            low, high = both[:rows, k * HALF : k * HALF + LANES], both[rows:, k * HALF : k * HALF + LANES]
            if low.shape[1] < LANES:
                spare = jnp.zeros((rows, LANES - low.shape[1]), F32)
                low, high = (jnp.concatenate([v, spare], axis=1) for v in (low, high))
            joined = [jnp.where(lane < HALF, low, shifted(high, HALF)), jnp.where(lane < HALF, shifted(low, HALF), high)]
            for b, across in zip(members[k : k + 2], joined):
                across_ref[b, at, :] = jnp.concatenate(split(across), axis=1)


def row_pass(start, row_band_ref, across_ref, images_ref, pitch):
    count = across_ref.shape[0]
    size = row_band_ref.shape[1]
    window = pl.ds(pl.multiple_of(start, 16), LANES)
    spare = jnp.zeros((LANES, LANES), BF16)
    for b in range(count):
        across = across_ref[b, window, :]
        under = jnp.concatenate([across[:, :LANES], spare], axis=1)
        both = lax.dot_general(
            row_band_ref[b], jnp.concatenate([across, under], axis=0), NN, preferred_element_type=F32
        )
        images_ref[pl.ds(b * pitch + start, size), :] = both[:, :LANES] + both[:, LANES:]


def make_weight(srow_ref, scol_ref, cov_ref, root_ref):
    _, rows, cols = root_ref.shape
    stamps = srow_ref.shape[1]
    at = iota((cols, stamps), 0) - scol_ref[...]
    cols_in = jnp.where((at >= 0) & (at < S), cov_ref[...].astype(F32), 0.0).astype(BF16)
    at = iota((rows, stamps), 0) - srow_ref[...]
    rows_in = jnp.where((at >= 0) & (at < S), 1.0, 0.0).astype(BF16)
    root = jnp.sqrt(lax.dot_general(rows_in, cols_in, NT, preferred_element_type=F32))
    root_ref[0] = root
    root_ref[1] = root * (2.0 * iota((rows, 1), 0).astype(F32) / rows - 1.0)


def gram(start, size, root_ref, images_ref, total_ref, pitch, total):
    cols = images_ref.shape[1]
    xi = xi_row(cols, total)
    plain, across, down = [], [], []
    for j in range(size):
        y = start + j
        feature = jnp.concatenate(
            [images_ref[pl.ds(first * pitch + y, 8, stride=pitch), :] for first in range(0, GROUP, 8)], axis=0
        )
        scaled = feature * root_ref[0, pl.ds(y, 1), :]
        plain.append(scaled)
        across.append(scaled * xi)
        down.append(feature * root_ref[1, pl.ds(y, 1), :])
    feats = jnp.concatenate([jnp.concatenate(v, axis=1) for v in (plain, across, down)], axis=0)
    high, low = split(feats)
    both = jnp.concatenate([high, low], axis=0)
    total_ref[...] += lax.dot_general(high, both, NT, preferred_element_type=F32)


def combine(total_ref):
    side = 3 * GROUP
    spare = jnp.zeros((side, LANES - side), F32)
    sums = total_ref[...]
    mixed = jnp.concatenate([sums[:, side:], spare], axis=1)
    turned = jnp.transpose(jnp.concatenate([mixed, jnp.zeros((LANES - side, LANES), F32)], axis=0))
    return jnp.concatenate([sums[:, :side], spare], axis=1) + (mixed + turned[:side])


def solve(normal, count):
    side = 3 * GROUP
    row, col = iota((side, LANES), 0), iota((side, LANES), 1)

    def used(k):
        return ((k % GROUP < count) & (k < side)) | (k == count)

    rhs = normal[:, count + 1 : count + 2]
    system = jnp.where(used(row) & used(col), normal, 0.0) + ridge_weight * jnp.where(row == col, 1.0, 0.0)
    system = jnp.where((col == side) & used(row), rhs, system)
    unknowns = [k for k in range(side) if (k % GROUP < count) or k == count]
    scale = jnp.zeros((side, LANES), F32)
    for first in range(0, len(unknowns), BLOCK):
        block = unknowns[first : first + BLOCK]
        columns = [jnp.broadcast_to(system[:, p : p + 1], (side, LANES)) for p in block]
        for k, p in enumerate(block):
            column = columns[k]
            inverse = 1.0 / column[p : p + 1, :]
            scale = jnp.where(row == p, inverse, scale)
            factor = jnp.where(row == p, 0.0, column)
            for later in range(k + 1, len(block)):
                columns[later] = columns[later] - factor * (columns[later][p : p + 1, :] * inverse)
            system = system - factor * (system[p : p + 1, :] * inverse)
    return jnp.broadcast_to(system[:, side : side + 1], (side, LANES)) * scale


def apply(coefs, images_ref, science_ref, out_ref, pitch, count, total):
    _, rows, cols = science_ref.shape
    xi = xi_row(cols, total)
    wide = lambda k: jnp.broadcast_to(coefs[k : k + 1, :], (8, cols))
    flat = [wide(b) + wide(GROUP + b) * xi for b in range(count)]
    slope = [wide(2 * GROUP + b) for b in range(count)]
    constant = wide(count)
    step = 4 if rows % 32 == 0 else 1

    def body(turn, carry):
        for k in range(step):
            start = pl.multiple_of((turn * step + k) * 8, 8)
            eta = 2.0 * (start + iota((8, cols), 0)).astype(F32) / rows - 1.0
            field = constant
            for b in range(count):
                field = field + images_ref[pl.ds(b * pitch + start, 8), :] * (flat[b] + slope[b] * eta)
            out_ref[0, pl.ds(start, 8), :] = science_ref[0, pl.ds(start, 8), :] - field
        return carry

    lax.fori_loop(0, rows // (8 * step), body, 0)


def remote(source, target, send, recv, epoch, tile):
    return pltpu.make_async_remote_copy(
        src_ref=source,
        dst_ref=target,
        send_sem=send,
        recv_sem=recv,
        device_id={"epoch": epoch, "tile": tile},
        device_id_type=pl.DeviceIdType.MESH,
    )


def kernel(total, top, pitch, template_in, science_in, rowp_in, colp_in, cov_in, srow_in, scol_in, out_ref,
           science_ref, rowp_ref, colp_ref, cov_ref, srow_ref, scol_ref,
           slots, pack, edges, across_ref, parts, mine, images_ref, root_ref, total_ref, profile_ref,
           row_band_ref, col_band_ref, slot_send, slot_recv, edge_send, edge_recv, side_send, side_recv,
           part_send, part_recv, load_sem):
    count, taps = rowp_ref.shape
    _, rows, cols = science_ref.shape
    epochs, own_rows, _ = slots.shape
    tiles = parts.shape[0]
    pieces = slot_recv.shape[1]
    size = row_band_ref.shape[1]
    epoch, tile = lax.axis_index("epoch"), lax.axis_index("tile")

    loads = [
        pltpu.make_async_copy(source, target, load_sem.at[k])
        for k, (source, target) in enumerate(
            [
                (template_in, slots.at[epoch]),
                (rowp_in, rowp_ref),
                (colp_in, colp_ref),
                (cov_in, cov_ref),
                (srow_in, srow_ref),
                (scol_in, scol_ref),
                (science_in, science_ref),
            ]
        )
    ]
    for load in loads:
        load.start()
    barrier = pltpu.get_barrier_semaphore()
    ahead, behind = epoch < epochs - 1, epoch > 0

    def greet(e, t):
        pl.semaphore_signal(barrier, inc=1, device_id={"epoch": e, "tile": t}, device_id_type=pl.DeviceIdType.MESH)

    for t in range(1, tiles):
        greet(epoch, lax.rem(tile + t, tiles))

    @pl.when(behind)
    def _():
        greet(epoch - 1, tile)

    @pl.when(ahead)
    def _():
        greet(epoch + 1, tile)

    loads[0].wait()
    flipped = jnp.transpose(slots[epoch])
    pack[0] = flipped[:EDGE]
    pack[1] = flipped[cols - EDGE :]
    pl.semaphore_wait(barrier, tiles - 1 + behind.astype(jnp.int32) + ahead.astype(jnp.int32))

    def block_copy(direction, source, piece):
        part = pl.ds(piece * (own_rows // pieces), own_rows // pieces)
        return remote(slots.at[source, part], slots.at[source, part], slot_send.at[direction, source, piece],
                      slot_recv.at[source, piece], epoch + 2 * direction - 1, tile)

    def edge_copy(direction, source):
        return remote(edges.at[source], edges.at[source], edge_send.at[direction, source], edge_recv.at[source],
                      epoch + 2 * direction - 1, tile)

    def side_copy(side):
        place = pl.ds((1 - side) * EDGE, EDGE)
        return remote(pack.at[side], edges.at[epoch, place], side_send.at[side], side_recv.at[1 - side],
                      epoch, tile + 2 * side - 1)

    has_left, has_right = tile > 0, tile < tiles - 1
    for direction, there in ((0, behind), (1, ahead)):

        @pl.when(there)
        def _():
            for piece in range(pieces):
                block_copy(direction, epoch, piece).start()

    for side, there in ((0, has_left), (1, has_right)):

        @pl.when(there)
        def _():
            side_copy(side).start()

        @pl.when(jnp.logical_not(there))
        def _():
            edges[epoch, side * EDGE : (side + 1) * EDGE, :] = jnp.zeros((EDGE, own_rows), F32)

    for load in loads[1:]:
        load.wait()
    make_bands(rowp_ref, colp_ref, profile_ref, row_band_ref, col_band_ref, top - taps // 2)
    high = across_ref.shape[1]
    across_ref[:, :top, :] = jnp.zeros((count, top, 2 * cols), BF16)
    across_ref[:, top + rows :, :] = jnp.zeros((count, high - top - rows, 2 * cols), BF16)

    for side, there in ((0, has_left), (1, has_right)):

        @pl.when(there)
        def _():
            side_copy(1 - side).wait_recv()

    for direction, there in ((0, behind), (1, ahead)):

        @pl.when(there)
        def _():
            edge_copy(direction, epoch).start()

    make_weight(srow_ref, scol_ref, cov_ref, root_ref)
    images_ref[pl.ds(count * pitch, rows), :] = jnp.ones((rows, cols), F32)
    images_ref[pl.ds((count + 1) * pitch, rows), :] = science_ref[0]
    for spare in range(count + 2, GROUP):
        images_ref[pl.ds(spare * pitch, rows), :] = jnp.zeros((rows, cols), F32)
    total_ref[...] = jnp.zeros_like(total_ref)

    each = size // own_rows
    middle = jnp.zeros((cols - 2 * EDGE, own_rows), F32)

    def columns(chunk):
        owns = [slots[chunk * each + k] for k in range(each)]
        sides = [jnp.transpose(jnp.concatenate([edges[chunk * each + k], middle], axis=0)) for k in range(each)]
        at = pl.ds(pl.multiple_of(top + chunk * size, 16), size)
        column_pass(jnp.concatenate(owns, axis=0), jnp.concatenate(sides, axis=0), at, taps, col_band_ref, across_ref)

    def chunk_work(chunk):
        start = pl.multiple_of(chunk * size, 16)
        row_pass(start, row_band_ref, across_ref, images_ref, pitch)
        gram(start, size, root_ref, images_ref, total_ref, pitch, total)

    def arrive(source, onward):
        direction = jnp.int32(onward)
        for piece in range(pieces):
            block_copy(direction, source, piece).wait_recv()

            @pl.when(ahead if onward else behind)
            def _():
                block_copy(direction, source, piece).start()

        edge_copy(direction, source).wait_recv()

        @pl.when(ahead if onward else behind)
        def _():
            edge_copy(direction, source).start()

    def step(d, carry):
        was_low, was_high = carry
        left, right = epoch - d, epoch + d
        has_before, has_after = (left >= 0) & (d > 0), (right < epochs) & (d > 0)

        @pl.when(has_before)
        def _():
            arrive(left, 1)

        @pl.when(has_after)
        def _():
            arrive(right, 0)

        if each > 1:
            return carry

        def fresh(k, carry):
            columns(jnp.where((k == 0) & (left >= 0), left, right))
            return carry

        lax.fori_loop(0, jnp.where(d == 0, 1, has_before.astype(jnp.int32) + has_after.astype(jnp.int32)), fresh, 0)
        low, high = jnp.maximum(left, 0), jnp.minimum(right, epochs - 1)
        low, high = jnp.where(low > 0, low + 1, low), jnp.where(high < epochs - 1, high, high + 1)
        low, high = jnp.where(low < high, low, epoch), jnp.where(low < high, high, epoch)
        under = was_low - low

        def ready(k, carry):
            chunk_work(jnp.where(k < under, was_low - 1 - k, was_high + k - under))
            return carry

        lax.fori_loop(0, under + high - was_high, ready, 0)
        return low, high

    lax.fori_loop(0, epochs, step, (epoch, epoch))
    if each > 1:

        def fresh_chunk(chunk, carry):
            columns(chunk)
            return carry

        def ready_chunk(chunk, carry):
            chunk_work(chunk)
            return carry

        lax.fori_loop(0, rows // size, fresh_chunk, 0)
        lax.fori_loop(0, rows // size, ready_chunk, 0)

    normal = combine(total_ref)
    side = 3 * GROUP
    normal = normal[: side // 2] + shifted(normal[side // 2 :], HALF)
    mine[...] = normal

    def part_copy(t, source):
        return remote(mine, parts.at[source], part_send.at[t], part_recv.at[source],
                      epoch, lax.rem(tile + t, tiles))

    for t in range(1, tiles):
        part_copy(t, tile).start()
    for t in range(1, tiles):
        source = lax.rem(tile + tiles - t, tiles)
        part_copy(t, source).wait_recv()
        normal = normal + parts[source]
    for t in range(1, tiles):
        part_copy(t, tile).wait_send()

    for s, there in ((0, has_left), (1, has_right)):

        @pl.when(there)
        def _():
            side_copy(s).wait_send()

    for direction, there in ((0, behind), (1, ahead)):

        def sent(source, carry):
            for piece in range(pieces):
                block_copy(direction, source, piece).wait_send()
            edge_copy(direction, source).wait_send()
            return carry

        @pl.when(there)
        def _():
            lax.fori_loop(*((0, epoch + 1) if direction else (epoch, epochs)), sent, 0)

    lane = iota((1, LANES), 1)
    normal = jnp.concatenate(
        [jnp.where(lane < HALF, normal, 0.0), jnp.where(lane < HALF, shifted(normal, HALF), 0.0)], axis=0
    )
    coefs = solve(normal, count)
    apply(coefs, images_ref, science_ref, out_ref, pitch, count, total)


def local(template, science, row_profiles, col_profiles, coverage, stamp_rows, stamp_cols):
    count, taps = row_profiles.shape
    rows, cols = science.shape[1:]
    own_rows = template.shape[0]
    tiles, epochs = lax.axis_size("tile"), lax.axis_size("epoch")
    top = -(-(taps // 2) // 16) * 16
    size = chunk_rows(rows, own_rows, taps - 1 + top - taps // 2)
    pitch = rows + 4
    pieces = PIECES if own_rows % (8 * PIECES) == 0 else 1
    vmem = pl.BlockSpec(memory_space=pltpu.VMEM)
    dma = pltpu.SemaphoreType.DMA
    operands = (
        template,
        science,
        row_profiles,
        col_profiles,
        coverage,
        stamp_rows.reshape(1, -1),
        stamp_cols.reshape(1, -1),
    )
    return pl.pallas_call(
        functools.partial(kernel, cols * tiles, top, pitch),
        out_shape=jax.ShapeDtypeStruct(science.shape, F32),
        in_specs=[pl.BlockSpec(memory_space=pl.ANY)] * 7,
        out_specs=vmem,
        scratch_shapes=[
            pltpu.VMEM(science.shape, F32),
            pltpu.VMEM(row_profiles.shape, F32),
            pltpu.VMEM(col_profiles.shape, F32),
            pltpu.VMEM(coverage.shape, jnp.int32),
            pltpu.VMEM((1, stamp_rows.shape[0]), jnp.int32),
            pltpu.VMEM((1, stamp_cols.shape[0]), jnp.int32),
            pltpu.VMEM((epochs, own_rows, cols), F32),
            pltpu.VMEM((2, EDGE, own_rows), F32),
            pltpu.VMEM((epochs, 2 * EDGE, own_rows), F32),
            pltpu.VMEM((count, rows - size + LANES, 2 * cols), BF16),
            pltpu.VMEM((tiles, 3 * GROUP // 2, LANES), F32),
            pltpu.VMEM((3 * GROUP // 2, LANES), F32),
            pltpu.VMEM((GROUP * pitch, cols), F32),
            pltpu.VMEM((2, rows, cols), F32),
            pltpu.VMEM((3 * GROUP, 6 * GROUP), F32),
            pltpu.VMEM((2, GROUP, 2 * LANES), F32),
            pltpu.VMEM((count, size, 2 * LANES), BF16),
            pltpu.VMEM((count, HALF, 2 * LANES), BF16),
            dma((2, epochs, pieces)),
            dma((epochs, pieces)),
            dma((2, epochs)),
            dma((epochs,)),
            dma((2,)),
            dma((2,)),
            dma((tiles,)),
            dma((tiles,)),
            dma((7,)),
        ],
        compiler_params=pltpu.CompilerParams(
            collective_id=0, has_side_effects=True, vmem_limit_bytes=48 * 2**20
        ),
    )(*(pltpu.with_memory_space_constraint(operand, pltpu.HBM) for operand in operands))


def solution(mesh):
    in_specs = (
        P(("patch", "epoch"), "tile"),
        P(("patch", "epoch"), None, "tile"),
        P(),
        P(),
        P(("patch", "epoch"), "tile"),
        P(("patch", "tile")),
        P(("patch", "tile")),
    )
    out_specs = P(("patch", "epoch"), None, "tile")
    return jax.shard_map(local, mesh=mesh, in_specs=in_specs, out_specs=out_specs, check_vma=False)
```

time: 28.5 us -> 25.3 us (0.89)
  Pallas kernels: 26.7 us -> 24.4 us
  local copies, waits for them, and re-layouts: 1.62 us -> 0.68 us
    pallas_call x1, Pallas kernels: 26.7 us -> 24.4 us  [local(): pl.pallas_call(functools.partial(kernel, cols * tiles, top, pitch), out_s...]
    unnamed x1, local copies, waits for them, and re-layouts: 1.62 us -> 0.68 us
where the time goes in v1:
time: 25.3 us; the launch traced here: 25.1 us
  Pallas kernels  24.4 us (96%)
  local copies, waits for them, and re-layouts  0.68 us (3%)
    pallas_call x1, Pallas kernels, local(): pl.pallas_call(functools.partial(kernel, cols * tiles, top, pitch), out_s...  24.4 us
    unnamed x1, local copies, waits for them, and re-layouts  0.68 us

profile of v1, /device:TPU:0, one launch (start us, length us, event | category | flops | bytes accessed | tf_op | source)
XLA Modules:
  0.0 25.1 jit_solution(15038570144071060946)
XLA Ops:
  0.0 24.4 %shard_map.73 = f32[1,384,128]{2,1,0:T(8,128)S(1)} custom-call(f32[96,128]{1,0:T(8,128)} %template_in.1, f32[1,384,128]{2,1,0:T(8,128)} %science_in.1, f32[12,21]{1,0:T(8,128)} %rowp_in.1, f32[12,21]{1,0:T(8,128)} %colp_in.1, s32[1,64]{1,0:T(1,128)} %cov_in.1, s32[1,64]{1,0:T(1,128)} %bitcast.2, s32[1,64]{1,0:T(1,128)} %bitcast.3), custom_call_target="tpu_custom_call" | custom-call | tf_op jit(solution)/shard_map/pallas_call | solution.py:466
  24.4 0.7 %copy.9 = f32[1,384,128]{2,1,0:T(8,128)} copy(f32[1,384,128]{2,1,0:T(8,128)S(1)} %shard_map.73) | data formatting | bytes 393216

commit v2 on v1

v2 whole, which is shorter than its diff:
```python
import functools

import jax
import jax.numpy as jnp
from jax import lax
from jax.experimental import pallas as pl
from jax.experimental.pallas import tpu as pltpu
from jax.sharding import PartitionSpec as P

S = 32
GROUP = 16
EDGE = 16
LANES = 128
HALF = LANES // 2
BLOCK = 8
SIDE = 40
TURN = 16
FOLD = 24
DUAL = 48
BOTH = 80
ridge_weight = 1.0
F32 = jnp.float32
BF16 = jnp.bfloat16
NT = (((1,), (1,)), ((), ()))
NN = (((1,), (0,)), ((), ()))


def split(value):
    high = value.astype(BF16)
    return high, (value - high.astype(F32)).astype(BF16)


def iota(shape, axis):
    return lax.broadcasted_iota(jnp.int32, shape, axis)


def shifted(value, turn):
    turn %= value.shape[1]
    return pltpu.roll(value, turn, 1) if turn else value


def toeplitz(profile_row, rows, turn=0):
    width = profile_row.shape[1]
    base = pltpu.roll(jnp.broadcast_to(profile_row, (8, width)), 0, 1, stride=1, stride_axis=0)
    return jnp.concatenate([shifted(base, turn + first) for first in range(0, rows, 8)], axis=0)


def xi_row(cols, total):
    start = lax.axis_index("tile") * cols
    return 2.0 * (start + iota((1, cols), 1)).astype(F32) / total - 1.0


def chunk_rows(rows, own, extra):
    sizes = [r for r in range(16, LANES - extra + 1, 16) if rows % r == 0 and r % own == 0]
    return max(sizes)


def make_bands(rowp_ref, colp_ref, profile_ref, row_band_ref, col_band_ref, shift):
    count, taps = rowp_ref.shape
    half = taps // 2
    profile_ref[...] = jnp.zeros_like(profile_ref)
    high, low = (part.astype(F32) for part in split(rowp_ref[...]))
    profile_ref[0, :count, shift : shift + taps] = high
    profile_ref[0, :count, LANES + shift : LANES + shift + taps] = low
    flip = jnp.where(iota((taps, taps), 0) + iota((taps, taps), 1) == taps - 1, 1.0, 0.0).astype(BF16)
    for k, part in enumerate(split(colp_ref[...])):
        profile_ref[1 + k, :count, :taps] = lax.dot_general(part, flip, NN, preferred_element_type=F32)
    gap = jnp.zeros((LANES - 6 * EDGE, LANES), BF16)
    for b in range(count):
        row_band_ref[b] = toeplitz(profile_ref[0, b : b + 1, :], row_band_ref.shape[1]).astype(BF16)
        parts = []
        for k in (1, 2):
            tall = toeplitz(profile_ref[k, b : b + 1, :], LANES + 2 * EDGE, -half - EDGE)[:, :LANES].astype(BF16)
            beside = jnp.concatenate([tall[:EDGE], tall[EDGE + LANES :]], axis=0)
            parts.append((tall[EDGE : EDGE + LANES], beside))
        (high, near_high), (low, near_low) = parts
        at = pl.ds((b % 2) * LANES, LANES)
        column = jnp.concatenate([high, high, low, near_high, near_high, near_low, gap], axis=0)
        col_band_ref[b // 2, :, at] = column


def column_pass(own, beside, at, col_band_ref, across_ref):
    count = across_ref.shape[0]
    lane = iota((1, LANES), 1)
    high, low = split(own)
    near = jnp.where(lane < 2 * EDGE, beside, 0.0)
    near_high = near.astype(BF16).astype(F32)
    near_low = near - near_high
    near = near_high + shifted(near_low, 2 * EDGE) + shifted(near_high, 4 * EDGE)
    terms = jnp.concatenate([high, low, high, near.astype(BF16)], axis=1)
    for pair in range(0, count, 2):
        both = lax.dot_general(terms, col_band_ref[pair // 2], NN, preferred_element_type=F32)
        for k, b in enumerate(range(pair, min(pair + 2, count))):
            across_ref[b, at, :] = jnp.concatenate(split(both[:, k * LANES : (k + 1) * LANES]), axis=1)


def row_pass(start, row_band_ref, across_ref, images_ref, pitch):
    count = across_ref.shape[0]
    size = row_band_ref.shape[1]
    window = pl.ds(pl.multiple_of(start, 16), LANES)
    spare = jnp.zeros((LANES, LANES), BF16)
    for b in range(count):
        across = across_ref[b, window, :]
        under = jnp.concatenate([across[:, :LANES], spare], axis=1)
        both = lax.dot_general(
            row_band_ref[b], jnp.concatenate([across, under], axis=0), NN, preferred_element_type=F32
        )
        images_ref[pl.ds(b * pitch + start, size), :] = both[:, :LANES] + both[:, LANES:]


def make_weight(srow_ref, scol_ref, cov_ref, root_ref, total):
    _, rows, cols = root_ref.shape
    stamps = srow_ref.shape[1]
    at = iota((cols, stamps), 0) - scol_ref[...]
    cols_in = jnp.where((at >= 0) & (at < S), cov_ref[...].astype(F32), 0.0).astype(BF16)
    at = iota((rows, stamps), 0) - srow_ref[...]
    rows_in = jnp.where((at >= 0) & (at < S), 1.0, 0.0).astype(BF16)
    root = jnp.sqrt(lax.dot_general(rows_in, cols_in, NT, preferred_element_type=F32))
    root_ref[0] = root
    root_ref[1] = root * xi_row(cols, total)
    root_ref[2] = root * (2.0 * iota((rows, 1), 0).astype(F32) / rows - 1.0)


def gram(start, size, root_ref, images_ref, first_ref, second_ref, pitch):
    upper = iota((8, images_ref.shape[1]), 0) < 4

    def row(j):
        y = start + j
        low, high, cross = (images_ref[pl.ds(k * pitch + y, 8, stride=pitch), :] for k in (0, 8, 4))
        plain, by_xi, by_eta = (jnp.broadcast_to(root_ref[k, pl.ds(y, 1), :], low.shape) for k in range(3))
        body = jnp.concatenate([low * plain, high * plain, low * by_xi, low * by_eta], axis=0)
        return body, jnp.where(upper, high, cross) * jnp.where(upper, by_xi, by_eta)

    def terms(first, last):
        body, rest = (jnp.concatenate(v, axis=1) for v in zip(*[row(j) for j in range(first, last)]))
        high, low = split(body)
        rest = jnp.concatenate([rest, rest - rest.astype(BF16).astype(F32)], axis=0).astype(BF16)
        short = jnp.concatenate([high, rest], axis=0)
        return short, jnp.concatenate([short, low], axis=0)

    first, second = first_ref[...], second_ref[...]
    for turn in range(0, size, TURN):
        short, whole = terms(turn, turn + TURN // 2)
        first = first + lax.dot_general(short, whole, NT, preferred_element_type=F32)
        short, whole = terms(turn + TURN // 2, turn + TURN)
        second = second + lax.dot_general(whole, short, NT, preferred_element_type=F32)
    first_ref[...], second_ref[...] = first, second


def combine(first_ref, second_ref):
    def pad(value, rows=SIDE):
        value = jnp.concatenate([value, jnp.zeros((value.shape[0], LANES - value.shape[1]), F32)], axis=1)
        if rows == value.shape[0]:
            return value
        return jnp.concatenate([value, jnp.zeros((rows - value.shape[0], LANES), F32)], axis=0)

    first, second = first_ref[:SIDE], second_ref[:, :SIDE]
    mixed = jnp.concatenate([first[:, DUAL:], first[:, SIDE:DUAL]], axis=1)
    mixed = mixed + jnp.concatenate([second[DUAL:], second[SIDE:DUAL]], axis=0)
    turned = jnp.transpose(pad(mixed, LANES))[:SIDE]
    return pad(first[:, :SIDE] + second[:SIDE]) + (pad(mixed) + turned)


def place(kind, b):
    if kind == 0:
        return b
    return (8 + 8 * kind + b) if b < 8 else (28 + 4 * kind + b - 8)


def solve(normal, count):
    side = SIDE
    row, col = iota((side, LANES), 0), iota((side, LANES), 1)
    unknowns = sorted([place(kind, b) for kind in range(3) for b in range(count)] + [count])

    def used(k):
        spare = [p for p in range(side) if p not in unknowns]
        keep = k < side
        for p in spare:
            keep = keep & (k != p)
        return keep

    rhs = normal[:, count + 1 : count + 2]
    system = jnp.where(used(row) & used(col), normal, 0.0) + ridge_weight * jnp.where(row == col, 1.0, 0.0)
    system = jnp.where((col == side) & used(row), rhs, system)
    scale = jnp.zeros((side, LANES), F32)
    for first in range(0, len(unknowns), BLOCK):
        block = unknowns[first : first + BLOCK]
        columns = [jnp.broadcast_to(system[:, p : p + 1], (side, LANES)) for p in block]
        for k, p in enumerate(block):
            column = columns[k]
            inverse = 1.0 / column[p : p + 1, :]
            scale = jnp.where(row == p, inverse, scale)
            factor = jnp.where(row == p, 0.0, column)
            for later in range(k + 1, len(block)):
                columns[later] = columns[later] - factor * (columns[later][p : p + 1, :] * inverse)
            system = system - factor * (system[p : p + 1, :] * inverse)
    return jnp.broadcast_to(system[:, side : side + 1], (side, LANES)) * scale


def apply(coefs, images_ref, science_ref, out_ref, pitch, count, total):
    _, rows, cols = science_ref.shape
    xi = xi_row(cols, total)
    wide = lambda k: jnp.broadcast_to(coefs[k : k + 1, :], (8, cols))
    flat = [wide(b) + wide(place(1, b)) * xi for b in range(count)]
    slope = [wide(place(2, b)) for b in range(count)]
    constant = wide(count)
    step = 4 if rows % 32 == 0 else 1

    def body(turn, carry):
        for k in range(step):
            start = pl.multiple_of((turn * step + k) * 8, 8)
            eta = 2.0 * (start + iota((8, cols), 0)).astype(F32) / rows - 1.0
            field = constant
            for b in range(count):
                field = field + images_ref[pl.ds(b * pitch + start, 8), :] * (flat[b] + slope[b] * eta)
            out_ref[0, pl.ds(start, 8), :] = science_ref[0, pl.ds(start, 8), :] - field
        return carry

    lax.fori_loop(0, rows // (8 * step), body, 0)


def remote(source, target, send, recv, epoch, tile):
    return pltpu.make_async_remote_copy(
        src_ref=source,
        dst_ref=target,
        send_sem=send,
        recv_sem=recv,
        device_id={"epoch": epoch, "tile": tile},
        device_id_type=pl.DeviceIdType.MESH,
    )


def kernel(total, top, pitch, template_in, science_in, rowp_in, colp_in, cov_in, srow_in, scol_in, out_ref,
           science_ref, rowp_ref, colp_ref, cov_ref, srow_ref, scol_ref,
           slots, pack, edges, across_ref, parts, mine, images_ref, root_ref, first_ref, second_ref, profile_ref,
           row_band_ref, col_band_ref, slot_send, slot_recv, edge_send, edge_recv,
           part_send, part_recv, load_sem, hello):
    count, taps = rowp_ref.shape
    _, rows, cols = science_ref.shape
    epochs, own_rows, _ = slots.shape
    tiles = parts.shape[0]
    size = row_band_ref.shape[1]
    epoch, tile = lax.axis_index("epoch"), lax.axis_index("tile")

    loads = [
        pltpu.make_async_copy(source, target, load_sem.at[k])
        for k, (source, target) in enumerate(
            [
                (template_in, slots.at[epoch]),
                (rowp_in, rowp_ref),
                (colp_in, colp_ref),
                (cov_in, cov_ref),
                (srow_in, srow_ref),
                (scol_in, scol_ref),
                (science_in, science_ref),
            ]
        )
    ]
    for load in loads:
        load.start()
    barrier = pltpu.get_barrier_semaphore()
    has_left, has_right = tile > 0, tile < tiles - 1

    def greet(semaphore, e, t):
        pl.semaphore_signal(semaphore, inc=1, device_id={"epoch": e, "tile": t}, device_id_type=pl.DeviceIdType.MESH)

    for t in range(1, tiles):
        greet(barrier, epoch, lax.rem(tile + t, tiles))

    def greet_above(target, carry):
        greet(barrier, target, tile)

        @pl.when(has_left)
        def _():
            greet(barrier, target, tile - 1)

        @pl.when(has_right)
        def _():
            greet(barrier, target, tile + 1)

        return carry

    lax.fori_loop(epoch + 1, epochs, greet_above, 0)
    loads[0].wait()
    flipped = jnp.transpose(slots[epoch])
    pack[0] = flipped[:EDGE]
    pack[1] = flipped[cols - EDGE :]
    around = 1 + has_left.astype(jnp.int32) + has_right.astype(jnp.int32)
    pl.semaphore_wait(barrier, tiles - 1 + epoch * around)

    def announce(target, carry):
        greet(hello.at[epoch], target, tile)
        return carry

    lax.fori_loop(0, epoch, announce, 0)

    def block_copy(target, source):
        return remote(template_in, slots.at[source], slot_send.at[target], slot_recv.at[source], target, tile)

    def edge_copy(target, side, source):
        place = pl.ds((1 - side) * EDGE, EDGE)
        return remote(pack.at[side], edges.at[source, place], edge_send.at[side, target], edge_recv.at[1 - side, source],
                      target, tile + 2 * side - 1)

    def send(target, carry):
        for side, there in ((0, has_left), (1, has_right)):

            @pl.when(there)
            def _():
                edge_copy(target, side, epoch).start()

        @pl.when(target != epoch)
        def _():
            block_copy(target, epoch).start()

        return carry

    def send_up(target):
        @pl.when(target < epochs)
        def _():
            pl.semaphore_wait(hello.at[target], 1)
            send(target, 0)

    lax.fori_loop(0, epoch + 1, send, 0)

    for side, there in ((0, has_left), (1, has_right)):

        @pl.when(jnp.logical_not(there))
        def _():
            edges[:, side * EDGE : (side + 1) * EDGE, :] = jnp.zeros((epochs, EDGE, own_rows), F32)

    for load in loads[1:]:
        load.wait()
    make_bands(rowp_ref, colp_ref, profile_ref, row_band_ref, col_band_ref, top - taps // 2)
    high = across_ref.shape[1]
    send_up(epoch + 1)
    across_ref[:, :top, :] = jnp.zeros((count, top, 2 * cols), BF16)
    across_ref[:, top + rows :, :] = jnp.zeros((count, high - top - rows, 2 * cols), BF16)

    make_weight(srow_ref, scol_ref, cov_ref, root_ref, total)
    images_ref[pl.ds(count * pitch, rows), :] = jnp.ones((rows, cols), F32)
    images_ref[pl.ds((count + 1) * pitch, rows), :] = science_ref[0]
    for spare in range(count + 2, GROUP):
        images_ref[pl.ds(spare * pitch, rows), :] = jnp.zeros((rows, cols), F32)
    first_ref[...] = jnp.zeros_like(first_ref)
    second_ref[...] = jnp.zeros_like(second_ref)

    each = size // own_rows
    middle = jnp.zeros((cols - 2 * EDGE, own_rows), F32)

    def columns(chunk):
        owns = [slots[chunk * each + k] for k in range(each)]
        sides = [jnp.transpose(jnp.concatenate([edges[chunk * each + k], middle], axis=0)) for k in range(each)]
        at = pl.ds(pl.multiple_of(top + chunk * size, 16), size)
        column_pass(jnp.concatenate(owns, axis=0), jnp.concatenate(sides, axis=0), at, col_band_ref, across_ref)

    def chunk_work(chunk):
        start = pl.multiple_of(chunk * size, 16)
        row_pass(start, row_band_ref, across_ref, images_ref, pitch)
        gram(start, size, root_ref, images_ref, first_ref, second_ref, pitch)

    def arrive(source):
        @pl.when(source != epoch)
        def _():
            block_copy(epoch, source).wait_recv()

        for side, there in ((0, has_left), (1, has_right)):

            @pl.when(there)
            def _():
                edge_copy(epoch, 1 - side, source).wait_recv()

    def step(d, carry):
        was_low, was_high = carry
        left, right = epoch - d, epoch + d
        has_before, has_after = (left >= 0) & (d > 0), right < epochs

        send_up(right + 2)

        @pl.when(has_before)
        def _():
            arrive(left)

        @pl.when(has_after)
        def _():
            arrive(right)

        if each > 1:
            return carry

        def fresh(k, carry):
            columns(jnp.where((k == 0) & has_before, left, right))
            return carry

        lax.fori_loop(0, has_before.astype(jnp.int32) + has_after.astype(jnp.int32), fresh, 0)
        low, high = jnp.maximum(left, 0), jnp.minimum(right, epochs - 1)
        low, high = jnp.where(low > 0, low + 1, low), jnp.where(high < epochs - 1, high, high + 1)
        low, high = jnp.where(low < high, low, epoch), jnp.where(low < high, high, epoch)
        under = was_low - low

        def ready(k, carry):
            chunk_work(jnp.where(k < under, was_low - 1 - k, was_high + k - under))
            return carry

        lax.fori_loop(0, under + high - was_high, ready, 0)
        return low, high

    lax.fori_loop(0, epochs, step, (epoch, epoch))
    if each > 1:

        def fresh_chunk(chunk, carry):
            columns(chunk)
            return carry

        def ready_chunk(chunk, carry):
            chunk_work(chunk)
            return carry

        lax.fori_loop(0, rows // size, fresh_chunk, 0)
        lax.fori_loop(0, rows // size, ready_chunk, 0)

    normal = combine(first_ref, second_ref)
    under = jnp.concatenate([normal[FOLD:], jnp.zeros((2 * FOLD - SIDE, LANES), F32)], axis=0)
    normal = normal[:FOLD] + shifted(under, HALF)
    mine[...] = normal

    def part_copy(t, source):
        return remote(mine, parts.at[source], part_send.at[t], part_recv.at[source],
                      epoch, lax.rem(tile + t, tiles))

    for t in range(1, tiles):
        part_copy(t, tile).start()
    for t in range(1, tiles):
        source = lax.rem(tile + tiles - t, tiles)
        part_copy(t, source).wait_recv()
        normal = normal + parts[source]
    for t in range(1, tiles):
        part_copy(t, tile).wait_send()

    def sent(target, carry):
        @pl.when(target != epoch)
        def _():
            block_copy(target, epoch).wait_send()

        for side, there in ((0, has_left), (1, has_right)):

            @pl.when(there)
            def _():
                edge_copy(target, side, epoch).wait_send()

        return carry

    lax.fori_loop(0, epochs, sent, 0)
    lane = iota((1, LANES), 1)
    normal = jnp.concatenate(
        [jnp.where(lane < HALF, normal, 0.0), jnp.where(lane < HALF, shifted(normal, HALF), 0.0)[: SIDE - FOLD]], axis=0
    )
    coefs = solve(normal, count)
    apply(coefs, images_ref, science_ref, out_ref, pitch, count, total)


def local(template, science, row_profiles, col_profiles, coverage, stamp_rows, stamp_cols):
    count, taps = row_profiles.shape
    rows, cols = science.shape[1:]
    own_rows = template.shape[0]
    tiles, epochs = lax.axis_size("tile"), lax.axis_size("epoch")
    top = -(-(taps // 2) // 16) * 16
    size = chunk_rows(rows, own_rows, taps - 1 + top - taps // 2)
    pitch = rows + 4
    vmem = pl.BlockSpec(memory_space=pltpu.VMEM)
    dma = pltpu.SemaphoreType.DMA
    operands = (
        template,
        science,
        row_profiles,
        col_profiles,
        coverage,
        stamp_rows.reshape(1, -1),
        stamp_cols.reshape(1, -1),
    )
    return pl.pallas_call(
        functools.partial(kernel, cols * tiles, top, pitch),
        out_shape=jax.ShapeDtypeStruct(science.shape, F32),
        in_specs=[pl.BlockSpec(memory_space=pl.ANY)] * 7,
        out_specs=vmem,
        scratch_shapes=[
            pltpu.VMEM(science.shape, F32),
            pltpu.VMEM(row_profiles.shape, F32),
            pltpu.VMEM(col_profiles.shape, F32),
            pltpu.VMEM(coverage.shape, jnp.int32),
            pltpu.VMEM((1, stamp_rows.shape[0]), jnp.int32),
            pltpu.VMEM((1, stamp_cols.shape[0]), jnp.int32),
            pltpu.VMEM((epochs, own_rows, cols), F32),
            pltpu.VMEM((2, EDGE, own_rows), F32),
            pltpu.VMEM((epochs, 2 * EDGE, own_rows), F32),
            pltpu.VMEM((count, rows - size + LANES, 2 * cols), BF16),
            pltpu.VMEM((tiles, FOLD, LANES), F32),
            pltpu.VMEM((FOLD, LANES), F32),
            pltpu.VMEM((GROUP * pitch, cols), F32),
            pltpu.VMEM((3, rows, cols), F32),
            pltpu.VMEM((DUAL, BOTH), F32),
            pltpu.VMEM((BOTH, DUAL), F32),
            pltpu.VMEM((3, GROUP, 2 * LANES), F32),
            pltpu.VMEM((count, size, 2 * LANES), BF16),
            pltpu.VMEM((-(-count // 2), 4 * LANES, 2 * LANES), BF16),
            dma((epochs,)),
            dma((epochs,)),
            dma((2, epochs)),
            dma((2, epochs)),
            dma((tiles,)),
            dma((tiles,)),
            dma((7,)),
            pltpu.SemaphoreType.REGULAR((epochs,)),
        ],
        compiler_params=pltpu.CompilerParams(
            collective_id=0, has_side_effects=True, vmem_limit_bytes=48 * 2**20
        ),
    )(*(pltpu.with_memory_space_constraint(operand, pltpu.HBM) for operand in operands))


def solution(mesh):
    in_specs = (
        P(("patch", "epoch"), "tile"),
        P(("patch", "epoch"), None, "tile"),
        P(),
        P(),
        P(("patch", "epoch"), "tile"),
        P(("patch", "tile")),
        P(("patch", "tile")),
    )
    out_specs = P(("patch", "epoch"), None, "tile")
    return jax.shard_map(local, mesh=mesh, in_specs=in_specs, out_specs=out_specs, check_vma=False)
```

time: 25.3 us -> 21.5 us (0.85)
  the two profiles are of different devices: /device:TPU:0 before, /device:TPU:17 now
where the time goes in v2:
time: 21.5 us; the launch traced here: 21.3 us
  Pallas kernels  20.6 us (96%)
  local copies, waits for them, and re-layouts  0.68 us (3%)
    pallas_call x1, Pallas kernels, local(): pl.pallas_call(functools.partial(kernel, cols * tiles, top, pitch), out_s...  20.6 us
    unnamed x1, local copies, waits for them, and re-layouts  0.68 us

profile of v2, /device:TPU:17, one launch (start us, length us, event | category | flops | bytes accessed | tf_op | source)
XLA Modules:
  0.0 21.3 jit_solution(17875807160491943896)
XLA Ops:
  0.0 20.6 %shard_map.73 = f32[1,384,128]{2,1,0:T(8,128)S(1)} custom-call(f32[96,128]{1,0:T(8,128)} %template_in.1, f32[1,384,128]{2,1,0:T(8,128)} %science_in.1, f32[12,21]{1,0:T(8,128)} %rowp_in.1, f32[12,21]{1,0:T(8,128)} %colp_in.1, s32[1,64]{1,0:T(1,128)} %cov_in.1, s32[1,64]{1,0:T(1,128)} %bitcast.2, s32[1,64]{1,0:T(1,128)} %bitcast.3), custom_call_target="tpu_custom_call" | custom-call | tf_op jit(solution)/shard_map/pallas_call | solution.py:481
  20.6 0.7 %copy.9 = f32[1,384,128]{2,1,0:T(8,128)} copy(f32[1,384,128]{2,1,0:T(8,128)S(1)} %shard_map.73) | data formatting | bytes 393216

commit v3 on v2

--- a/solution.py
+++ b/solution.py
@@ -12,9 +12,9 @@
 EDGE = 16
 LANES = 128
 HALF = LANES // 2
-BLOCK = 8
+BLOCK = 13
 SIDE = 40
-TURN = 16
+TURN = 8
 FOLD = 24
 DUAL = 48
 BOTH = 80
@@ -50,8 +50,8 @@
     return 2.0 * (start + iota((1, cols), 1)).astype(F32) / total - 1.0
 
 
-def chunk_rows(rows, own, extra):
-    sizes = [r for r in range(16, LANES - extra + 1, 16) if rows % r == 0 and r % own == 0]
+def unit_rows(rows, own, top):
+    sizes = [r for r in range(16, 2 * LANES // 3 - 2 * top + 1, 16) if rows % (2 * r) == 0 and 2 * r % own == 0]
     return max(sizes)
 
 
@@ -60,14 +60,16 @@
     half = taps // 2
     profile_ref[...] = jnp.zeros_like(profile_ref)
     high, low = (part.astype(F32) for part in split(rowp_ref[...]))
-    profile_ref[0, :count, shift : shift + taps] = high
-    profile_ref[0, :count, LANES + shift : LANES + shift + taps] = low
+    _, size, width = row_band_ref.shape
+    for k, part in enumerate((high, high, low)):
+        at = k * (width // 3) + shift
+        profile_ref[0, :count, at : at + taps] = part
     flip = jnp.where(iota((taps, taps), 0) + iota((taps, taps), 1) == taps - 1, 1.0, 0.0).astype(BF16)
     for k, part in enumerate(split(colp_ref[...])):
         profile_ref[1 + k, :count, :taps] = lax.dot_general(part, flip, NN, preferred_element_type=F32)
     gap = jnp.zeros((LANES - 6 * EDGE, LANES), BF16)
     for b in range(count):
-        row_band_ref[b] = toeplitz(profile_ref[0, b : b + 1, :], row_band_ref.shape[1]).astype(BF16)
+        row_band_ref[b] = toeplitz(profile_ref[0, b : b + 1, :], size)[:, :width].astype(BF16)
         parts = []
         for k in (1, 2):
             tall = toeplitz(profile_ref[k, b : b + 1, :], LANES + 2 * EDGE, -half - EDGE)[:, :LANES].astype(BF16)
@@ -94,18 +96,19 @@
             across_ref[b, at, :] = jnp.concatenate(split(both[:, k * LANES : (k + 1) * LANES]), axis=1)
 
 
-def row_pass(start, row_band_ref, across_ref, images_ref, pitch):
+def row_pass(starts, row_band_ref, across_ref, images_ref, pitch):
     count = across_ref.shape[0]
-    size = row_band_ref.shape[1]
-    window = pl.ds(pl.multiple_of(start, 16), LANES)
-    spare = jnp.zeros((LANES, LANES), BF16)
+    _, size, width = row_band_ref.shape
     for b in range(count):
-        across = across_ref[b, window, :]
-        under = jnp.concatenate([across[:, :LANES], spare], axis=1)
+        sides = []
+        for start in starts:
+            across = across_ref[b, pl.ds(start, width // 3), :]
+            sides.append(jnp.concatenate([across[:, :LANES], across[:, LANES:], across[:, :LANES]], axis=0))
         both = lax.dot_general(
-            row_band_ref[b], jnp.concatenate([across, under], axis=0), NN, preferred_element_type=F32
+            row_band_ref[b], jnp.concatenate(sides, axis=1), NN, preferred_element_type=F32
         )
-        images_ref[pl.ds(b * pitch + start, size), :] = both[:, :LANES] + both[:, LANES:]
+        for k, start in enumerate(starts):
+            images_ref[pl.ds(b * pitch + start, size), :] = both[:, k * LANES : (k + 1) * LANES]
 
 
 def make_weight(srow_ref, scol_ref, cov_ref, root_ref, total):
@@ -121,28 +124,29 @@
     root_ref[2] = root * (2.0 * iota((rows, 1), 0).astype(F32) / rows - 1.0)
 
 
-def gram(start, size, root_ref, images_ref, first_ref, second_ref, pitch):
+def gram(starts, size, root_ref, images_ref, first_ref, second_ref, pitch):
     upper = iota((8, images_ref.shape[1]), 0) < 4
 
-    def row(j):
-        y = start + j
+    def row(y):
         low, high, cross = (images_ref[pl.ds(k * pitch + y, 8, stride=pitch), :] for k in (0, 8, 4))
         plain, by_xi, by_eta = (jnp.broadcast_to(root_ref[k, pl.ds(y, 1), :], low.shape) for k in range(3))
         body = jnp.concatenate([low * plain, high * plain, low * by_xi, low * by_eta], axis=0)
         return body, jnp.where(upper, high, cross) * jnp.where(upper, by_xi, by_eta)
 
-    def terms(first, last):
-        body, rest = (jnp.concatenate(v, axis=1) for v in zip(*[row(j) for j in range(first, last)]))
+    def terms(start):
+        body, rest = (jnp.concatenate(v, axis=1) for v in zip(*[row(start + j) for j in range(TURN)]))
         high, low = split(body)
         rest = jnp.concatenate([rest, rest - rest.astype(BF16).astype(F32)], axis=0).astype(BF16)
         short = jnp.concatenate([high, rest], axis=0)
         return short, jnp.concatenate([short, low], axis=0)
 
     first, second = first_ref[...], second_ref[...]
-    for turn in range(0, size, TURN):
-        short, whole = terms(turn, turn + TURN // 2)
+    step = size * len(starts) // 2
+    near, far = starts[0], starts[0] + step if len(starts) == 1 else starts[1]
+    for turn in range(0, step, TURN):
+        short, whole = terms(near + turn)
         first = first + lax.dot_general(short, whole, NT, preferred_element_type=F32)
-        short, whole = terms(turn + TURN // 2, turn + TURN)
+        short, whole = terms(far + turn)
         second = second + lax.dot_general(whole, short, NT, preferred_element_type=F32)
     first_ref[...], second_ref[...] = first, second
 
@@ -295,7 +299,7 @@
     lax.fori_loop(0, epoch, announce, 0)
 
     def block_copy(target, source):
-        return remote(template_in, slots.at[source], slot_send.at[target], slot_recv.at[source], target, tile)
+        return remote(slots.at[source], slots.at[source], slot_send.at[target], slot_recv.at[source], target, tile)
 
     def edge_copy(target, side, source):
         place = pl.ds((1 - side) * EDGE, EDGE)
@@ -345,19 +349,20 @@
     first_ref[...] = jnp.zeros_like(first_ref)
     second_ref[...] = jnp.zeros_like(second_ref)
 
-    each = size // own_rows
+    each = 2 * size // own_rows
+    chunks = rows // (2 * size)
     middle = jnp.zeros((cols - 2 * EDGE, own_rows), F32)
 
     def columns(chunk):
         owns = [slots[chunk * each + k] for k in range(each)]
         sides = [jnp.transpose(jnp.concatenate([edges[chunk * each + k], middle], axis=0)) for k in range(each)]
-        at = pl.ds(pl.multiple_of(top + chunk * size, 16), size)
+        at = pl.ds(pl.multiple_of(top + chunk * 2 * size, 16), 2 * size)
         column_pass(jnp.concatenate(owns, axis=0), jnp.concatenate(sides, axis=0), at, col_band_ref, across_ref)
 
-    def chunk_work(chunk):
-        start = pl.multiple_of(chunk * size, 16)
-        row_pass(start, row_band_ref, across_ref, images_ref, pitch)
-        gram(start, size, root_ref, images_ref, first_ref, second_ref, pitch)
+    def work(units):
+        starts = [pl.multiple_of(unit * size, 16) for unit in units]
+        row_pass(starts, row_band_ref, across_ref, images_ref, pitch)
+        gram(starts, size, root_ref, images_ref, first_ref, second_ref, pitch)
 
     def arrive(source):
         @pl.when(source != epoch)
@@ -371,41 +376,50 @@
                 edge_copy(epoch, 1 - side, source).wait_recv()
 
     def step(d, carry):
-        was_low, was_high = carry
-        left, right = epoch - d, epoch + d
-        has_before, has_after = (left >= 0) & (d > 0), right < epochs
-
-        send_up(right + 2)
-
-        @pl.when(has_before)
-        def _():
-            arrive(left)
-
-        @pl.when(has_after)
-        def _():
-            arrive(right)
-
-        if each > 1:
+        @pl.when(d > 0)
+        def _():
+            send_up(epoch + d + 1)
+
+        def side(k, carry):
+            right = (k + (2 * epoch < epochs).astype(jnp.int32)) % 2 == 0
+            source = epoch + jnp.where(right, d, -d)
+            valid = (source >= 0) & (source < epochs) & ((d > 0) | (k == 0))
+
+            @pl.when(valid)
+            def _():
+                arrive(source)
+
+            if each == 1:
+
+                @pl.when(valid)
+                def _():
+                    columns(source)
+
+                far = (epoch + d >= epochs - 1) & (epoch - d <= 0)
+                other = epoch + jnp.where(right, -d, d)
+                done = far & ((k == 1) | (other < 0) | (other >= epochs)) & (d > 0)
+                lone = (epoch == 0) | (epoch == epochs - 1)
+
+                def ready(turn, carry):
+                    chunk = jnp.where(turn == 0, source + jnp.where(right, 0, 1), 0)
+                    work((jnp.where(turn == 0, 2 * chunk - 1, 0), jnp.where(turn == 0, 2 * chunk, 2 * chunks - 1)))
+                    return carry
+
+                pairs = (d > 0).astype(jnp.int32) + (done & jnp.logical_not(lone)).astype(jnp.int32)
+                lax.fori_loop(0, jnp.where(valid, pairs, 0), ready, 0)
+
+                def margin(turn, carry):
+                    work((jnp.where((turn == 0) & (source == 0), 0, 2 * chunks - 1),))
+                    return carry
+
+                margins = (source == 0).astype(jnp.int32) + (source == epochs - 1).astype(jnp.int32)
+                lax.fori_loop(0, jnp.where(valid & lone, margins, 0), margin, 0)
             return carry
 
-        def fresh(k, carry):
-            columns(jnp.where((k == 0) & has_before, left, right))
-            return carry
-
-        lax.fori_loop(0, has_before.astype(jnp.int32) + has_after.astype(jnp.int32), fresh, 0)
-        low, high = jnp.maximum(left, 0), jnp.minimum(right, epochs - 1)
-        low, high = jnp.where(low > 0, low + 1, low), jnp.where(high < epochs - 1, high, high + 1)
-        low, high = jnp.where(low < high, low, epoch), jnp.where(low < high, high, epoch)
-        under = was_low - low
-
-        def ready(k, carry):
-            chunk_work(jnp.where(k < under, was_low - 1 - k, was_high + k - under))
-            return carry
-
-        lax.fori_loop(0, under + high - was_high, ready, 0)
-        return low, high
-
-    lax.fori_loop(0, epochs, step, (epoch, epoch))
+        lax.fori_loop(0, 2, side, 0)
+        return carry
+
+    lax.fori_loop(0, epochs, step, 0)
     if each > 1:
 
         def fresh_chunk(chunk, carry):
@@ -413,11 +427,16 @@
             return carry
 
         def ready_chunk(chunk, carry):
-            chunk_work(chunk)
+            work((2 * chunk - 1, 2 * chunk))
             return carry
 
-        lax.fori_loop(0, rows // size, fresh_chunk, 0)
-        lax.fori_loop(0, rows // size, ready_chunk, 0)
+        def margin_unit(turn, carry):
+            work((turn * (2 * chunks - 1),))
+            return carry
+
+        lax.fori_loop(0, chunks, fresh_chunk, 0)
+        lax.fori_loop(1, chunks, ready_chunk, 0)
+        lax.fori_loop(0, 2, margin_unit, 0)
 
     normal = combine(first_ref, second_ref)
     under = jnp.concatenate([normal[FOLD:], jnp.zeros((2 * FOLD - SIDE, LANES), F32)], axis=0)
@@ -465,7 +484,7 @@
     own_rows = template.shape[0]
     tiles, epochs = lax.axis_size("tile"), lax.axis_size("epoch")
     top = -(-(taps // 2) // 16) * 16
-    size = chunk_rows(rows, own_rows, taps - 1 + top - taps // 2)
+    size = unit_rows(rows, own_rows, top)
     pitch = rows + 4
     vmem = pl.BlockSpec(memory_space=pltpu.VMEM)
     dma = pltpu.SemaphoreType.DMA
@@ -493,7 +512,7 @@
             pltpu.VMEM((epochs, own_rows, cols), F32),
             pltpu.VMEM((2, EDGE, own_rows), F32),
             pltpu.VMEM((epochs, 2 * EDGE, own_rows), F32),
-            pltpu.VMEM((count, rows - size + LANES, 2 * cols), BF16),
+            pltpu.VMEM((count, rows + 2 * top, 2 * cols), BF16),
             pltpu.VMEM((tiles, FOLD, LANES), F32),
             pltpu.VMEM((FOLD, LANES), F32),
             pltpu.VMEM((GROUP * pitch, cols), F32),
@@ -501,7 +520,7 @@
             pltpu.VMEM((DUAL, BOTH), F32),
             pltpu.VMEM((BOTH, DUAL), F32),
             pltpu.VMEM((3, GROUP, 2 * LANES), F32),
-            pltpu.VMEM((count, size, 2 * LANES), BF16),
+            pltpu.VMEM((count, size, 3 * (size + 2 * top)), BF16),
             pltpu.VMEM((-(-count // 2), 4 * LANES, 2 * LANES), BF16),
             dma((epochs,)),
             dma((epochs,)),

time: 21.5 us -> 20.2 us (0.940)
  the two profiles are of different devices: /device:TPU:17 before, /device:TPU:0 now
where the time goes in v3:
time: 20.2 us; the launch traced here: 20.1 us
  Pallas kernels  19.4 us (96%)
  local copies, waits for them, and re-layouts  0.68 us (3%)
    pallas_call x1, Pallas kernels, local(): pl.pallas_call(functools.partial(kernel, cols * tiles, top, pitch), out_s...  19.4 us
    unnamed x1, local copies, waits for them, and re-layouts  0.68 us

profile of v3, /device:TPU:0, one launch (start us, length us, event | category | flops | bytes accessed | tf_op | source)
XLA Modules:
  0.0 20.1 jit_solution(8778221454048454206)
XLA Ops:
  0.0 19.4 %shard_map.73 = f32[1,384,128]{2,1,0:T(8,128)S(1)} custom-call(f32[96,128]{1,0:T(8,128)} %template_in.1, f32[1,384,128]{2,1,0:T(8,128)} %science_in.1, f32[12,21]{1,0:T(8,128)} %rowp_in.1, f32[12,21]{1,0:T(8,128)} %colp_in.1, s32[1,64]{1,0:T(1,128)} %cov_in.1, s32[1,64]{1,0:T(1,128)} %bitcast.2, s32[1,64]{1,0:T(1,128)} %bitcast.3), custom_call_target="tpu_custom_call" | custom-call | tf_op jit(solution)/shard_map/pallas_call | solution.py:500
  19.4 0.7 %copy.9 = f32[1,384,128]{2,1,0:T(8,128)} copy(f32[1,384,128]{2,1,0:T(8,128)S(1)} %shard_map.73) | data formatting | bytes 393216

commit v4 on v3

--- a/solution.py
+++ b/solution.py
@@ -307,16 +307,16 @@
                       target, tile + 2 * side - 1)
 
     def send(target, carry):
+        @pl.when(target != epoch)
+        def _():
+            block_copy(target, epoch).start()
+
         for side, there in ((0, has_left), (1, has_right)):
 
             @pl.when(there)
             def _():
                 edge_copy(target, side, epoch).start()
 
-        @pl.when(target != epoch)
-        def _():
-            block_copy(target, epoch).start()
-
         return carry
 
     def send_up(target):
@@ -325,7 +325,8 @@
             pl.semaphore_wait(hello.at[target], 1)
             send(target, 0)
 
-    lax.fori_loop(0, epoch + 1, send, 0)
+    shift = jnp.where(epoch == epochs - 1, jnp.maximum(epochs - 2, 0), 0)
+    lax.fori_loop(0, epoch + 1, lambda k, carry: send(lax.rem(k + shift, epoch + 1), carry), 0)
 
     for side, there in ((0, has_left), (1, has_right)):
 
@@ -453,29 +454,32 @@
         source = lax.rem(tile + tiles - t, tiles)
         part_copy(t, source).wait_recv()
         normal = normal + parts[source]
-    for t in range(1, tiles):
-        part_copy(t, tile).wait_send()
-
-    def sent(target, carry):
-        @pl.when(target != epoch)
-        def _():
-            block_copy(target, epoch).wait_send()
-
-        for side, there in ((0, has_left), (1, has_right)):
-
-            @pl.when(there)
-            def _():
-                edge_copy(target, side, epoch).wait_send()
-
-        return carry
-
-    lax.fori_loop(0, epochs, sent, 0)
+
+
     lane = iota((1, LANES), 1)
     normal = jnp.concatenate(
         [jnp.where(lane < HALF, normal, 0.0), jnp.where(lane < HALF, shifted(normal, HALF), 0.0)[: SIDE - FOLD]], axis=0
     )
     coefs = solve(normal, count)
     apply(coefs, images_ref, science_ref, out_ref, pitch, count, total)
+
+    for t in range(1, tiles):
+        part_copy(t, tile).wait_send()
+
+    def sent(target, carry):
+        @pl.when(target != epoch)
+        def _():
+            block_copy(target, epoch).wait_send()
+
+        for side, there in ((0, has_left), (1, has_right)):
+
+            @pl.when(there)
+            def _():
+                edge_copy(target, side, epoch).wait_send()
+
+        return carry
+
+    lax.fori_loop(0, epochs, sent, 0)
 
 
 def local(template, science, row_profiles, col_profiles, coverage, stamp_rows, stamp_cols):

time: 20.2 us -> 18.9 us (0.936)
  the two profiles are of different devices: /device:TPU:0 before, /device:TPU:9 now
where the time goes in v4:
time: 18.9 us; the launch traced here: 18.8 us
  Pallas kernels  18.1 us (96%)
  local copies, waits for them, and re-layouts  0.68 us (4%)
    pallas_call x1, Pallas kernels, local(): pl.pallas_call(functools.partial(kernel, cols * tiles, top, pitch), out_s...  18.1 us
    unnamed x1, local copies, waits for them, and re-layouts  0.68 us

profile of v4, /device:TPU:9, one launch (start us, length us, event | category | flops | bytes accessed | tf_op | source)
XLA Modules:
  0.0 18.8 jit_solution(11886473678801918532)
XLA Ops:
  0.0 18.1 %shard_map.73 = f32[1,384,128]{2,1,0:T(8,128)S(1)} custom-call(f32[96,128]{1,0:T(8,128)} %template_in.1, f32[1,384,128]{2,1,0:T(8,128)} %science_in.1, f32[12,21]{1,0:T(8,128)} %rowp_in.1, f32[12,21]{1,0:T(8,128)} %colp_in.1, s32[1,64]{1,0:T(1,128)} %cov_in.1, s32[1,64]{1,0:T(1,128)} %bitcast.2, s32[1,64]{1,0:T(1,128)} %bitcast.3), custom_call_target="tpu_custom_call" | custom-call | tf_op jit(solution)/shard_map/pallas_call | solution.py:504
  18.1 0.7 %copy.9 = f32[1,384,128]{2,1,0:T(8,128)} copy(f32[1,384,128]{2,1,0:T(8,128)S(1)} %shard_map.73) | data formatting | bytes 393216

commit v5 on v4

--- a/solution.py
+++ b/solution.py
@@ -208,7 +208,7 @@
     flat = [wide(b) + wide(place(1, b)) * xi for b in range(count)]
     slope = [wide(place(2, b)) for b in range(count)]
     constant = wide(count)
-    step = 4 if rows % 32 == 0 else 1
+    step = 8 if rows % 64 == 0 else 1
 
     def body(turn, carry):
         for k in range(step):
@@ -338,7 +338,6 @@
         load.wait()
     make_bands(rowp_ref, colp_ref, profile_ref, row_band_ref, col_band_ref, top - taps // 2)
     high = across_ref.shape[1]
-    send_up(epoch + 1)
     across_ref[:, :top, :] = jnp.zeros((count, top, 2 * cols), BF16)
     across_ref[:, top + rows :, :] = jnp.zeros((count, high - top - rows, 2 * cols), BF16)
 
@@ -347,6 +346,7 @@
     images_ref[pl.ds((count + 1) * pitch, rows), :] = science_ref[0]
     for spare in range(count + 2, GROUP):
         images_ref[pl.ds(spare * pitch, rows), :] = jnp.zeros((rows, cols), F32)
+    send_up(epoch + 1)
     first_ref[...] = jnp.zeros_like(first_ref)
     second_ref[...] = jnp.zeros_like(second_ref)
 
@@ -396,25 +396,17 @@
                 def _():
                     columns(source)
 
-                far = (epoch + d >= epochs - 1) & (epoch - d <= 0)
-                other = epoch + jnp.where(right, -d, d)
-                done = far & ((k == 1) | (other < 0) | (other >= epochs)) & (d > 0)
-                lone = (epoch == 0) | (epoch == epochs - 1)
-
-                def ready(turn, carry):
-                    chunk = jnp.where(turn == 0, source + jnp.where(right, 0, 1), 0)
-                    work((jnp.where(turn == 0, 2 * chunk - 1, 0), jnp.where(turn == 0, 2 * chunk, 2 * chunks - 1)))
-                    return carry
-
-                pairs = (d > 0).astype(jnp.int32) + (done & jnp.logical_not(lone)).astype(jnp.int32)
-                lax.fori_loop(0, jnp.where(valid, pairs, 0), ready, 0)
+                @pl.when(valid & (d > 0))
+                def _():
+                    chunk = source + jnp.where(right, 0, 1)
+                    work((2 * chunk - 1, 2 * chunk))
 
                 def margin(turn, carry):
                     work((jnp.where((turn == 0) & (source == 0), 0, 2 * chunks - 1),))
                     return carry
 
                 margins = (source == 0).astype(jnp.int32) + (source == epochs - 1).astype(jnp.int32)
-                lax.fori_loop(0, jnp.where(valid & lone, margins, 0), margin, 0)
+                lax.fori_loop(0, jnp.where(valid, margins, 0), margin, 0)
             return carry
 
         lax.fori_loop(0, 2, side, 0)
@@ -448,7 +440,7 @@
         return remote(mine, parts.at[source], part_send.at[t], part_recv.at[source],
                       epoch, lax.rem(tile + t, tiles))
 
-    for t in range(1, tiles):
+    for t in sorted(range(1, tiles), key=lambda t: -t * (tiles - t)):
         part_copy(t, tile).start()
     for t in range(1, tiles):
         source = lax.rem(tile + tiles - t, tiles)

time: 18.9 us -> 18.8 us (level)
  the two profiles are of different devices: /device:TPU:9 before, /device:TPU:25 now
where the time goes in v5:
time: 18.8 us; the launch traced here: 18.6 us
  Pallas kernels  18 us (96%)
  local copies, waits for them, and re-layouts  0.68 us (4%)
    pallas_call x1, Pallas kernels, local(): pl.pallas_call(functools.partial(kernel, cols * tiles, top, pitch), out_s...  18 us
    unnamed x1, local copies, waits for them, and re-layouts  0.68 us

profile of v5, /device:TPU:25, one launch (start us, length us, event | category | flops | bytes accessed | tf_op | source)
XLA Modules:
  0.0 18.6 jit_solution(4329600639288086494)
XLA Ops:
  0.0 18.0 %shard_map.73 = f32[1,384,128]{2,1,0:T(8,128)S(1)} custom-call(f32[96,128]{1,0:T(8,128)} %template_in.1, f32[1,384,128]{2,1,0:T(8,128)} %science_in.1, f32[12,21]{1,0:T(8,128)} %rowp_in.1, f32[12,21]{1,0:T(8,128)} %colp_in.1, s32[1,64]{1,0:T(1,128)} %cov_in.1, s32[1,64]{1,0:T(1,128)} %bitcast.2, s32[1,64]{1,0:T(1,128)} %bitcast.3), custom_call_target="tpu_custom_call" | custom-call | tf_op jit(solution)/shard_map/pallas_call | solution.py:496
  18.0 0.7 %copy.9 = f32[1,384,128]{2,1,0:T(8,128)} copy(f32[1,384,128]{2,1,0:T(8,128)S(1)} %shard_map.73) | data formatting | bytes 393216

commit v6 on v5

--- a/solution.py
+++ b/solution.py
@@ -392,12 +392,13 @@
 
             if each == 1:
 
-                @pl.when(valid)
+                @pl.when(valid & (d == 0))
                 def _():
                     columns(source)
 
                 @pl.when(valid & (d > 0))
                 def _():
+                    columns(source)
                     chunk = source + jnp.where(right, 0, 1)
                     work((2 * chunk - 1, 2 * chunk))
 

time: 18.8 us -> 18.8 us (level)
  no operation moved by 1% of the time
where the time goes in v6:
time: 18.8 us; the launch traced here: 18.6 us
  Pallas kernels  17.9 us (95%)
  local copies, waits for them, and re-layouts  0.68 us (4%)
    pallas_call x1, Pallas kernels, local(): pl.pallas_call(functools.partial(kernel, cols * tiles, top, pitch), out_s...  17.9 us
    unnamed x1, local copies, waits for them, and re-layouts  0.68 us

profile of v6, /device:TPU:25, one launch (start us, length us, event | category | flops | bytes accessed | tf_op | source)
XLA Modules:
  0.0 18.6 jit_solution(14208165688654731005)
XLA Ops:
  0.0 17.9 %shard_map.73 = f32[1,384,128]{2,1,0:T(8,128)S(1)} custom-call(f32[96,128]{1,0:T(8,128)} %template_in.1, f32[1,384,128]{2,1,0:T(8,128)} %science_in.1, f32[12,21]{1,0:T(8,128)} %rowp_in.1, f32[12,21]{1,0:T(8,128)} %colp_in.1, s32[1,64]{1,0:T(1,128)} %cov_in.1, s32[1,64]{1,0:T(1,128)} %bitcast.2, s32[1,64]{1,0:T(1,128)} %bitcast.3), custom_call_target="tpu_custom_call" | custom-call | tf_op jit(solution)/shard_map/pallas_call | solution.py:497
  17.9 0.7 %copy.9 = f32[1,384,128]{2,1,0:T(8,128)} copy(f32[1,384,128]{2,1,0:T(8,128)S(1)} %shard_map.73) | data formatting | bytes 393216
